TPU v7x, 128 devices: a whole 4x4x4 slice. The times are simulated.
128 devices in a mesh: slab: 64 (over z, y, x), tile: 2 (over core).
Axes of the slice: x: 4, y: 4, z: 4, core: 2. Of those that a mesh axis runs over, the one named last changes fastest.
Arguments:
- samples: float32 [64, 256, 32, 256], P('slab', None, 'tile'), may hold values from -6 to 6
- counts: int32 [64, 256, 32], P('slab', None, 'tile'), may hold values from 1 to 4
- w_in: float32 [64, 64, 256], P('slab'), may hold values from -0.75 to 0.75
- b_in: float32 [64, 256], P('slab'), may hold values from -3 to 3
- w_color: float32 [64, 256, 128], P('slab'), may hold values from -0.375 to 0.375
- b_color: float32 [64, 128], P('slab'), may hold values from -3 to 3
- w_density: float32 [64, 256], P('slab'), may hold values from -0.375 to 0.375
- b_density: float32 [64], P('slab'), may hold values from -1 to 1
- conv_a: bfloat16 [3, 3, 128, 128], replicated, may hold values from -0.1875 to 0.1875
- bias_a: float32 [128], replicated, may hold values from -3 to 3
- conv_b: bfloat16 [3, 3, 128, 128], replicated, may hold values from -0.1875 to 0.1875
- bias_b: float32 [128], replicated, may hold values from -3 to 3
Outputs:
- decoded: bfloat16 [256, 32, 128], P('slab', 'tile')
- front: float32 [64, 256, 32], P('slab', None, 'tile')
All inputs are finite; a program needn't handle non-finite values.
Results may differ from a plain program's by a relative error of at most 0.006.
Values may be sent and summed in bfloat16 or wider, within the bound.
No kernel may reach another device: no remote copies, remote signals or barrier semaphores. Data moves between devices by JAX's collectives and lax.ppermute only.
A program may use at most 128 MiB of HBM per device.

v0:
```python
import jax
import jax.numpy as jnp
from jax import lax
from jax.sharding import PartitionSpec as P

F = 64
K = 4


def padded_2(cells, sides, width):
    for axis, dim in sides:
        count = lax.axis_size(axis)
        ends = count - 1
        head = lax.slice_in_dim(cells, 0, width, axis=dim)
        tail = lax.slice_in_dim(cells, cells.shape[dim] - width, cells.shape[dim], axis=dim)
        cells = jnp.concatenate(
            [
                lax.ppermute(tail, axis, [(i, (i + 1) % count) for i in range(ends)]),
                cells,
                lax.ppermute(head, axis, [((i + 1) % count, i) for i in range(ends)]),
            ],
            axis=dim,
        )
    return cells


def prefix_2(part, axis, combine, identity):
    place = lax.axis_index(axis)
    gathered = lax.all_gather(part, axis)
    state = jnp.zeros_like(part) + jnp.asarray(identity, part.dtype)

    def one(turn, state):
        return combine(state, lax.dynamic_index_in_dim(gathered, turn, 0, False))

    return lax.fori_loop(0, place, one, state)


def hidden_units(inputs, w_in, b_in):
    shaped = inputs.reshape(inputs.shape[:-1] + (K, F))
    return jax.nn.relu(
        jnp.einsum("rwkf,fh->rwkh", shaped, w_in, precision=lax.Precision.HIGHEST) + b_in
    )


def densities(hidden_act, w_density, b_density, live_count):
    before = (
        jnp.einsum("rwkh,h->rwk", hidden_act, w_density, precision=lax.Precision.HIGHEST)
        + b_density
    )
    slots = lax.broadcasted_iota(jnp.int32, before.shape, 2)
    return jnp.where(slots < live_count[..., None], jax.nn.softplus(before), 0.0)


def sample_weights(density, front, total):
    scaled = density / total[..., None]
    earlier = jnp.cumsum(scaled, axis=2) - scaled
    return jnp.exp(-front[..., None] - earlier) * (1.0 - jnp.exp(-scaled))


def partial_image(hidden_act, weight, w_color, b_color):
    color = (
        jnp.einsum("rwkh,hc->rwkc", hidden_act, w_color, precision=lax.Precision.HIGHEST) + b_color
    )
    return jnp.einsum("rwk,rwkc->rwc", weight, color, precision=lax.Precision.HIGHEST)


def add_pair(earlier, later):
    return earlier + later


def convolve(padded, kernel, out_rows, out_cols):
    result = jnp.zeros((out_rows, out_cols, kernel.shape[3]), jnp.float32)
    for row_shift in range(3):
        for col_shift in range(3):
            window = padded[row_shift : row_shift + out_rows, col_shift : col_shift + out_cols]
            result = result + jnp.einsum(
                "rwc,cd->rwd",
                window,
                kernel[row_shift, col_shift],
                preferred_element_type=jnp.float32,
            )
    return result


def strip_edges(field):
    return padded_2(field, (("slab", 0), ("tile", 1)), 1)


def body(
    samples,
    counts,
    w_in,
    b_in,
    w_color,
    b_color,
    w_density,
    b_density,
    conv_a,
    bias_a,
    conv_b,
    bias_b,
):
    slab_count = lax.axis_size("slab")
    height = samples.shape[1]
    tile_cols = samples.shape[2]
    strip_rows = height // slab_count
    hidden_act = hidden_units(samples[0], w_in[0], b_in[0])
    density = densities(hidden_act, w_density[0], b_density[0], counts[0])
    depth = jnp.sum(density, axis=2)
    prefix = prefix_2(depth, "slab", add_pair, jnp.zeros_like(depth))
    total = lax.psum(depth, "slab")
    front = prefix / total
    weight = sample_weights(density, front, total)
    image = lax.psum_scatter(
        partial_image(hidden_act, weight, w_color[0], b_color[0]),
        "slab",
        scatter_dimension=0,
        tiled=True,
    ).astype(jnp.bfloat16)
    first_pad = strip_edges(image)
    hidden_map = jax.nn.relu(convolve(first_pad, conv_a, strip_rows, tile_cols) + bias_a).astype(
        jnp.bfloat16
    )
    second_pad = strip_edges(hidden_map)
    decoded = (convolve(second_pad, conv_b, strip_rows, tile_cols) + bias_b).astype(jnp.bfloat16)
    return (decoded, front[None])


def solution(mesh):
    in_specs = (
        P("slab", None, "tile", None),
        P("slab", None, "tile"),
        P("slab", None, None),
        P("slab", None),
        P("slab", None, None),
        P("slab", None),
        P("slab", None),
        P("slab"),
        P(),
        P(),
        P(),
        P(),
    )
    out_specs = (P("slab", "tile", None), P("slab", None, "tile"))
    return jax.shard_map(body, mesh=mesh, in_specs=in_specs, out_specs=out_specs, check_vma=False)
```

profile of v0, /device:TPU:1, one launch (start us, length us, event | category | flops | bytes accessed | tf_op | source)
XLA Modules:
  0.0 851.4 jit_solution(13505761106247215219)
XLA Ops:
  7.2 0.0 copy-start
  7.2 0.0 copy-start.4
  7.2 0.0 all-gather.3.cloned.1.call-start
  7.2 5.3 copy.24
  12.5 15.6 %fusion.32 = f32[256,16,4,256]{3,0,2,1:T(8,128)S(1)} fusion(f32[256,16,4,64]{0,3,2,1:T(8,128)} %bitcast.147, f32[1,64,256]{2,1,0:T(8,128)S(1)} %copy-done.4), kind=kOutput, calls=%fused_computation.42 | convolution fusion | flops 3221225472 | bytes 21037056 | tf_op jit(solution)/shard_map/rwkf,fh->rwkh/dot_general | solution.py:41
  28.1 5.7 copy-done.1
  33.8 0.0 copy-done.6
  33.8 15.2 %fusion.2 = f32[1,256,16,4]{0,1,3,2:T(8,128)} fusion(f32[256,16,4,256]{3,0,2,1:T(8,128)S(1)} %fusion.32, f32[256]{0:T(256)S(1)} %bitcast.153, f32[1,256]{1,0:T(1,128)S(1)} %copy-done.8), kind=kOutput, calls=%fused_computation.5 | convolution fusion | flops 58720256 | bytes 16844800 | tf_op jit(solution)/shard_map/rwkh,h->rwk/dot_general | solution.py:47
  49.1 5.2 copy.28
  54.9 0.0 copy-done.5
  55.0 0.7 fusion.111
  55.6 0.0 all-gather.3.cloned.1.call-update
  55.6 0.0 reduce-scatter.2.cloned.1.call-start
  55.7 296.8 %psum.7 = f32[256,16]{0,1:T(8,128)S(1)} all-reduce(f32[256,16]{0,1:T(8,128)} %fusion.111), channel_id=1, replica_groups=mesh['slab'=64,'tile'=2] {'slab'}, use_global_device_ids=true, to_apply=%region_3.4 | all-reduce | flops 4096 | bytes 32768 | tf_op jit(solution)/shard_map/psum | solution.py:111
  352.5 0.0 copy-done.7
  352.5 18.1 %broadcast_add_fusion = f32[256,16,4,128]{3,0,2,1:T(8,128)} fusion(f32[128]{0:T(128)S(1)} %bitcast.155, f32[256,16,4,256]{3,0,2,1:T(8,128)} %copy-done.1, f32[256]{0:T(256)S(1)} %bitcast.154, f32[1,256,128]{2,1,0:T(8,128)S(1)} %copy-done), kind=kOutput, calls=%fused_computation.12 | convolution fusion | flops 6452936704 | bytes 25298432 | tf_op jit(solution)/shard_map/rwkh,hc->rwkc/dot_general | solution.py:62
  370.6 1.5 copy.34
  372.1 0.6 divide_bitcast_fusion
  372.7 0.2 fusion.29
  372.9 1.1 copy.30
  374.0 0.0 copy-start.2
  374.0 0.0 copy-start.9
  374.1 0.0 copy-start.3
  374.1 0.0 copy-start.10
  374.1 35.2 %fusion.7 = f32[256,16,1,128]{3,2,1,0:T(1,128)} fusion(f32[256,16,4,1]{2,3,1,0:T(1,128)S(1)} %copy.30, f32[256,16,4,128]{3,0,2,1:T(8,128)} %broadcast_add_fusion), kind=kOutput, calls=%fused_computation.10 | convolution fusion | flops 25165824 | bytes 10551296 | tf_op jit(solution)/shard_map/rwk,rwkc->rwc/dot_general | solution.py:64
  409.3 0.0 reduce-scatter.2.cloned.1.call-update
  409.3 356.2 %reduce-scatter.2.cloned.1.call-done = f32[4,16,128]{2,1,0:T(8,128)} async-done(((f32[256,16,128]{2,1,0:T(8,128)}), f32[4,16,128]{2,1,0:T(8,128)}) %reduce-scatter.2.cloned.1.call-update) | async-done | bytes 32784 | tf_op jit(solution)/shard_map/reduce_scatter | solution.py:114
  765.5 0.8 convert_element_type.9
  766.3 1.3 collective-permute-start
  767.6 1.3 collective-permute-start.1
  768.9 0.1 fusion.58
  769.0 0.0 collective-permute-done
  769.0 3.3 collective-permute-done.1
  772.4 1.3 collective-permute-start.2
  773.7 56.3 %collective-permute-start.3 = (bf16[6,1,128]{2,1,0:T(2,128)(2,1)S(1)}, bf16[6,1,128]{2,1,0:T(2,128)(2,1)S(1)}, u32[]{:S(2)}, u32[]{:S(2)}) collective-permute-start(bf16[6,1,128]{2,1,0:T(2,128)(2,1)S(1)} %get-tuple-element.55), channel_id=1, source_target_pairs={{1,0},{3,2},{5,4},{7,6},{9,8},{11,10},{13,12},{15,14},{17,16},{19,... | collective-permute-start | bytes 4616 | tf_op jit(solution)/shard_map/ppermute | solution.py:20
  829.9 0.1 fusion.64
  830.1 0.1 fusion.53
  830.2 0.0 collective-permute-done.2
  830.2 0.5 collective-permute-done.3
  830.8 0.1 fusion.62
  830.9 0.1 fusion.51
  831.0 0.1 fusion.60
  831.1 0.1 fusion.55
  831.3 0.1 fusion.26
  831.4 0.1 fusion.27
  831.6 1.4 collective-permute-start.4
  833.0 1.3 collective-permute-start.5
  834.3 0.0 copy-done.3
  834.3 0.1 fusion.42
  834.4 0.0 collective-permute-done.4
  834.4 2.9 collective-permute-done.5
  837.3 1.3 collective-permute-start.6
  838.6 3.7 collective-permute-start.7
  842.3 0.1 fusion.48
  842.4 0.1 fusion.37
  842.6 0.0 collective-permute-done.6
  842.6 0.5 collective-permute-done.7
  843.1 0.1 fusion.46
  843.3 0.1 fusion.35
  843.4 0.1 fusion.44
  843.5 0.1 fusion.39
  843.7 0.1 fusion.18
  843.8 0.0 copy-done.10
  843.8 0.8 fusion.28
  (19 shorter events, 0.1 us)
Async XLA Ops:
  7.2 345.3 %copy-start = (f32[1,256,128]{2,1,0:T(8,128)S(1)}, f32[1,256,128]{2,1,0:T(8,128)}, u32[]{:S(2)}) copy-start(f32[1,256,128]{2,1,0:T(8,128)} %param.18) | copy-start | bytes 393220
  7.2 5.3 copy-start.4
  7.2 363.4 %all-gather.3.cloned.1.call-start = ((), (), s32[]{:S(2)}) async-start(), calls=%async_computation.2 | async-start | bytes 1064960 | tf_op jit(solution)/shard_map/all_gather | solution.py:29
  12.5 21.3 %copy-start.6 = (f32[1,256]{1,0:T(1,128)S(1)}, f32[1,256]{1,0:T(1,128)}, u32[]{:S(2)}) copy-start(f32[1,256]{1,0:T(1,128)} %param.17) | copy-start | bytes 3076
  12.5 21.3 %copy-start.8 = (f32[1,256]{1,0:T(1,128)S(1)}, f32[1,256]{1,0:T(1,128)}, u32[]{:S(2)}) copy-start(f32[1,256]{1,0:T(1,128)} %param.20) | copy-start | bytes 3076
  28.1 5.7 copy-start.1
  49.1 5.9 copy-start.5
  49.1 303.4 %copy-start.7 = (f32[1,128]{1,0:T(1,128)S(1)}, f32[1,128]{1,0:T(1,128)}, u32[]{:S(2)}) copy-start(f32[1,128]{1,0:T(1,128)} %param.19) | copy-start | bytes 1540
  55.6 709.9 %reduce-scatter.2.cloned.1.call-start = ((), (), s32[]{:S(2)}) async-start(), calls=%async_computation.1 | async-start | bytes 2129920 | tf_op jit(solution)/shard_map/reduce_scatter | solution.py:114
  374.0 394.9 %copy-start.2 = (bf16[3,3,128,128]{3,2,1,0:T(8,128)(2,1)S(1)}, bf16[3,3,128,128]{3,2,1,0:T(8,128)(2,1)}, u32[]{:S(2)}) copy-start(bf16[3,3,128,128]{3,2,1,0:T(8,128)(2,1)} %param.22) | copy-start | bytes 884740
  374.0 457.4 %copy-start.9 = (f32[128]{0:T(128)S(1)}, f32[128]{0:T(128)}, u32[]{:S(2)}) copy-start(f32[128]{0:T(128)} %param.23) | copy-start | bytes 1540
  374.1 460.2 %copy-start.3 = (bf16[3,3,128,128]{3,2,1,0:T(8,128)(2,1)S(1)}, bf16[3,3,128,128]{3,2,1,0:T(8,128)(2,1)}, u32[]{:S(2)}) copy-start(bf16[3,3,128,128]{3,2,1,0:T(8,128)(2,1)} %param.24) | copy-start | bytes 884740
  374.1 469.7 %copy-start.10 = (f32[128]{0:T(128)S(1)}, f32[128]{0:T(128)}, u32[]{:S(2)}) copy-start(f32[128]{0:T(128)} %param.25) | copy-start | bytes 1540
  766.3 2.7 collective-permute-start
  767.6 4.8 collective-permute-start.1
  772.4 57.8 %collective-permute-start.2 = (bf16[6,1,128]{2,1,0:T(2,128)(2,1)S(1)}, bf16[6,1,128]{2,1,0:T(2,128)(2,1)S(1)}, u32[]{:S(2)}, u32[]{:S(2)}) collective-permute-start(bf16[6,1,128]{2,1,0:T(2,128)(2,1)S(1)} %get-tuple-element.54), channel_id=1, source_target_pairs={{0,1},{2,3},{4,5},{6,7},{8,9},{10,11},{12,13},{14,15},{16,17},{18,... | collective-permute-start | bytes 4616 | tf_op jit(solution)/shard_map/ppermute | solution.py:18
  773.7 57.1 %collective-permute-start.3 = (bf16[6,1,128]{2,1,0:T(2,128)(2,1)S(1)}, bf16[6,1,128]{2,1,0:T(2,128)(2,1)S(1)}, u32[]{:S(2)}, u32[]{:S(2)}) collective-permute-start(bf16[6,1,128]{2,1,0:T(2,128)(2,1)S(1)} %get-tuple-element.55), channel_id=1, source_target_pairs={{1,0},{3,2},{5,4},{7,6},{9,8},{11,10},{13,12},{15,14},{17,16},{19,... | collective-permute-start | bytes 4616 | tf_op jit(solution)/shard_map/ppermute | solution.py:20
  831.6 2.8 collective-permute-start.4
  833.0 4.4 collective-permute-start.5
  837.3 5.2 collective-permute-start.6
  838.6 4.5 collective-permute-start.7
Sparse Core Ops, SparseCore 0:
  55.8 64.9 all-gather.2
  409.4 356.0 reduce-scatter.1
where the time goes:
time: 852 us; the launch traced here: 851 us
  waiting for transfers between devices  364 us (43%)
  blocking collectives  297 us (35%)
  matrix products  87.1 us (10%)
  starting transfers between devices  67.8 us (8%)
  local copies, waits for them, and re-layouts  18.9 us (2%)
  between operations  14.9 us (2%)
    reduce_scatter x1, waiting for transfers between devices, body(): lax.psum_scatter(partial_image(hidden_act, weight, w_color[0], b_color[0]...  356 us
    psum x1, blocking collectives, body(): total = lax.psum(depth, 'slab')  297 us
    ppermute x4, starting transfers between devices, padded_2(): lax.ppermute(head, axis, [((i + 1) % count, i) for i in range(ends)])  62.5 us
    dot_general x1, matrix products, partial_image(): jnp.einsum('rwk,rwkc->rwc', weight, color, precision=lax.Precision.HIGHEST)  35.2 us
    dot_general x1, matrix products, partial_image(): jnp.einsum('rwkh,hc->rwkc', hidden_act, w_color, precision=lax.Precision....  18.1 us
  transfers between devices with their start and end apart: 10, of which 5 were waited for; matrix products, arithmetic and copies ran while one was open for 2% of the time, Pallas kernels for 0%

commit v1 on v0

v1 whole, which is shorter than its diff:
```python
import jax
import jax.numpy as jnp
from jax import lax
from jax.experimental import pallas as pl
from jax.experimental.pallas import tpu as pltpu
from jax.sharding import PartitionSpec as P

F = 64
HID = 256
C = 128
K = 4
SLABS = 64
ROWS = 256
COLS = 16
RAYS = ROWS * COLS
LANES = 128
GROUPS = RAYS // LANES
BLOCK = 512
PER = BLOCK // LANES
STRIP = 4
BF = jnp.bfloat16
F32 = jnp.float32

NT = (((1,), (1,)), ((), ()))


def column(row, lanes):
    return jnp.broadcast_to(row, (lanes, row.shape[1])).T


def dense_kernel(x, counts, w_in, b_in, w_color, w_density, b_density,
                 color, density, depth, w_s, b_s, d_s, c_s, logit):
    step = pl.program_id(0)

    @pl.when(step == 0)
    def _():
        turned = w_in[0].T.astype(BF)
        w_s[...] = jnp.zeros_like(w_s)
        for k in range(K):
            w_s[k * HID:(k + 1) * HID, k * F:(k + 1) * F] = turned
        b_s[...] = column(b_in[...], LANES)
        d_s[...] = column(w_density[...], LANES)
        c_s[...] = w_color[0].T.astype(BF)

    rays = x[...].astype(BF)
    bias = jnp.concatenate([b_s[...]] * PER, axis=1)
    head = jnp.concatenate([d_s[...]] * PER, axis=1)
    for k in range(K):
        hidden = lax.dot_general(w_s[k * HID:(k + 1) * HID, :], rays, NT, preferred_element_type=F32)
        hidden = jnp.maximum(hidden + bias, 0.0)
        before = jnp.sum(hidden * head, axis=0, keepdims=True)
        for g in range(PER):
            logit[k, pl.ds(step * PER + g, 1), :] = before[:, g * LANES:(g + 1) * LANES]
        made = jnp.dot(c_s[...], hidden.astype(BF), preferred_element_type=F32)
        color[k] = made.astype(BF)

    @pl.when(step == pl.num_programs(0) - 1)
    def _():
        live = jnp.concatenate(
            [counts[0, pl.ds(a, GROUPS, stride=8), :] for a in range(8)], axis=1
        )
        total = jnp.zeros((GROUPS, LANES), F32)
        for k in range(K):
            pre = logit[k] + b_density[0]
            soft = jnp.maximum(pre, 0.0) + jnp.log1p(jnp.exp(-jnp.abs(pre)))
            soft = jnp.where(live > k, soft, 0.0)
            density[k] = soft
            total = total + soft
        depth[...] = jnp.broadcast_to(total.astype(BF)[None], depth.shape)


def weigh_kernel(depths, density, color, b_color, image, front, w_s, b_s):
    step = pl.program_id(0)

    @pl.when(step == 0)
    def _():
        place = lax.axis_index("slab")
        b_s[...] = column(b_color[...], LANES)

        def add(turn, state):
            total, ahead = state
            one = depths[turn].astype(F32)
            return total + one, ahead + jnp.where(turn < place, one, 0.0)

        zero = jnp.zeros((GROUPS, LANES), F32)
        total, ahead = lax.fori_loop(0, SLABS, add, (zero, zero), unroll=8)
        ahead = ahead / total
        for a in range(8):
            front[0, pl.ds(a, GROUPS, stride=8), :] = ahead[:, a * COLS:(a + 1) * COLS]
        passed = ahead
        for k in range(K):
            scaled = density[k] / total
            w_s[k] = jnp.exp(-passed) * (1.0 - jnp.exp(-scaled))
            passed = passed + scaled

    for g in range(PER):
        at = pl.ds(step * PER + g, 1)
        weights = [w_s[k, at, :] for k in range(K)]
        part = b_s[...] * (weights[0] + weights[1] + weights[2] + weights[3])
        for k in range(K):
            part = part + color[k, :, g * LANES:(g + 1) * LANES].astype(F32) * weights[k]
        image[g * LANES:(g + 1) * LANES, :] = part.T.astype(BF)


def sum_kernel(parts, strip, top, bottom):
    total = jnp.zeros((STRIP * COLS, C), F32)

    def add(turn, state):
        return state + parts[turn].astype(F32)

    total = lax.fori_loop(0, SLABS, add, total, unroll=8).astype(BF)
    strip[...] = total
    top[...] = total[:2 * COLS]
    bottom[...] = total[2 * COLS:]


PITCH = 32
EDGE = 8


def taps(field, rows):
    flat = field.reshape(-1, C)
    span = flat.shape[0]
    shifted = [pltpu.roll(flat, 1, 0).astype(BF), flat.astype(BF), pltpu.roll(flat, span - 1, 0).astype(BF)]
    return jnp.concatenate(
        [s[PITCH * r:PITCH * (r + rows)] for r in range(3) for s in shifted], axis=1
    )


def decode_kernel(strip, above, below, strip_p, above_p, below_p, conv_a, bias_a, conv_b, bias_b, out, patch):
    place = lax.axis_index("slab")
    tile = lax.axis_index("tile")
    first = place == 0
    last = place == SLABS - 1

    def whole(up, mid, down):
        up = jnp.where(first, 0.0, up[...].astype(F32))
        down = jnp.where(last, 0.0, down[...].astype(F32))
        return jnp.concatenate([up, mid[...].astype(F32), down], axis=0).reshape(STRIP + 4, COLS, C)

    own = whole(above, strip, below)
    other = whole(above_p, strip_p, below_p)
    patch[...] = jnp.zeros_like(patch)
    patch[:, EDGE:EDGE + COLS, :] = own
    patch[:, EDGE - 2:EDGE, :] = jnp.where(tile == 0, 0.0, other[:, COLS - 2:, :])
    patch[:, EDGE + COLS:EDGE + COLS + 2, :] = jnp.where(tile == 0, other[:, :2, :], 0.0)
    rows = STRIP + 2
    made = jnp.dot(taps(patch[...], rows), conv_a[...].reshape(9 * C, C), preferred_element_type=F32)
    made = jnp.maximum(made + bias_a[...], 0.0).astype(BF).astype(F32).reshape(rows, PITCH, C)
    row = lax.broadcasted_iota(jnp.int32, made.shape, 0) + (place * STRIP - 1)
    col = lax.broadcasted_iota(jnp.int32, made.shape, 1) + (tile * COLS - EDGE)
    inside = (row >= 0) & (row < ROWS) & (col >= 0) & (col < 2 * COLS)
    made = jnp.where(inside, made, 0.0)
    done = jnp.dot(taps(made, STRIP), conv_b[...].reshape(9 * C, C), preferred_element_type=F32) + bias_b[...]
    out[...] = done.reshape(STRIP, PITCH, C)[:, EDGE:EDGE + COLS, :].astype(BF)


def full(*shape):
    return pl.BlockSpec(shape, lambda i: (0,) * len(shape))


def body(samples, counts, w_in, b_in, w_color, b_color, w_density, b_density, conv_a, bias_a, conv_b, bias_b):
    vmem = pl.BlockSpec(memory_space=pltpu.VMEM)
    steps = RAYS // BLOCK
    color, density, depth = pl.pallas_call(
        dense_kernel,
        grid=(steps,),
        in_specs=[
            pl.BlockSpec((BLOCK, K * F), lambda i: (i, 0)),
            full(1, ROWS, COLS),
            full(1, F, HID),
            full(1, HID),
            full(1, HID, C),
            full(1, HID),
            pl.BlockSpec(memory_space=pltpu.SMEM),
        ],
        out_specs=[
            pl.BlockSpec((K, C, BLOCK), lambda i: (0, 0, i)),
            full(K, GROUPS, LANES),
            full(SLABS, GROUPS, LANES),
        ],
        out_shape=[
            jax.ShapeDtypeStruct((K, C, RAYS), BF),
            jax.ShapeDtypeStruct((K, GROUPS, LANES), F32),
            jax.ShapeDtypeStruct((SLABS, GROUPS, LANES), BF),
        ],
        scratch_shapes=[
            pltpu.VMEM((K * HID, K * F), BF),
            pltpu.VMEM((HID, LANES), F32),
            pltpu.VMEM((HID, LANES), F32),
            pltpu.VMEM((C, HID), BF),
            pltpu.VMEM((K, GROUPS, LANES), F32),
        ],
        name="dense",
    )(samples.reshape(RAYS, K * F), counts, w_in, b_in, w_color, w_density, b_density)

    depths = lax.all_to_all(depth, "slab", 0, 0, tiled=True)

    image, front = pl.pallas_call(
        weigh_kernel,
        grid=(steps,),
        in_specs=[
            full(SLABS, GROUPS, LANES),
            full(K, GROUPS, LANES),
            pl.BlockSpec((K, C, BLOCK), lambda i: (0, 0, i)),
            full(1, C),
        ],
        out_specs=[
            pl.BlockSpec((BLOCK, C), lambda i: (i, 0)),
            full(1, ROWS, COLS),
        ],
        out_shape=[
            jax.ShapeDtypeStruct((RAYS, C), BF),
            jax.ShapeDtypeStruct((1, ROWS, COLS), F32),
        ],
        scratch_shapes=[
            pltpu.VMEM((K, GROUPS, LANES), F32),
            pltpu.VMEM((C, LANES), F32),
        ],
        name="weigh",
    )(depths, density, color, b_color)

    parts = lax.all_to_all(image.reshape(SLABS, STRIP * COLS, C), "slab", 0, 0, tiled=True)

    strip, top, bottom = pl.pallas_call(
        sum_kernel,
        in_specs=[vmem],
        out_specs=[vmem] * 3,
        out_shape=[
            jax.ShapeDtypeStruct((STRIP * COLS, C), BF),
            jax.ShapeDtypeStruct((2 * COLS, C), BF),
            jax.ShapeDtypeStruct((2 * COLS, C), BF),
        ],
        name="gathered",
    )(parts)

    onward = [(i, (i + 1) % SLABS) for i in range(SLABS)]
    back = [(j, i) for i, j in onward]
    swap = [(0, 1), (1, 0)]
    above = lax.ppermute(bottom, "slab", onward)
    below = lax.ppermute(top, "slab", back)
    strip_p = lax.ppermute(strip, "tile", swap)
    above_p = lax.ppermute(above, "tile", swap)
    below_p = lax.ppermute(below, "tile", swap)

    decoded = pl.pallas_call(
        decode_kernel,
        in_specs=[vmem] * 10,
        out_specs=vmem,
        out_shape=jax.ShapeDtypeStruct((STRIP, COLS, C), BF),
        scratch_shapes=[pltpu.VMEM((STRIP + 4, PITCH, C), F32)],
        name="decode",
    )(strip, above, below, strip_p, above_p, below_p, conv_a, bias_a.reshape(1, C), conv_b, bias_b.reshape(1, C))
    return decoded, front


def solution(mesh):
    in_specs = (
        P("slab", None, "tile", None),
        P("slab", None, "tile"),
        P("slab", None, None),
        P("slab", None),
        P("slab", None, None),
        P("slab", None),
        P("slab", None),
        P("slab"),
        P(),
        P(),
        P(),
        P(),
    )
    out_specs = (P("slab", "tile", None), P("slab", None, "tile"))
    return jax.shard_map(body, mesh=mesh, in_specs=in_specs, out_specs=out_specs, check_vma=False)
```

time: 852 us -> 89.2 us (0.10)
  waiting for transfers between devices: 364 us -> 0.01 us
  blocking collectives: 297 us -> 46.2 us
  matrix products: 87.1 us -> 0 us
  starting transfers between devices: 67.8 us -> 12.6 us
  Pallas kernels: 0 us -> 24.8 us
  local copies, waits for them, and re-layouts: 18.9 us -> 3.64 us
  between operations: 14.9 us -> 1.33 us
    reduce_scatter x1 -> x0, waiting for transfers between devices: 356 us -> none  [body(): lax.psum_scatter(partial_image(hidden_act, weight, w_color[0], b_color[0]...]
    psum x1 -> x0, blocking collectives: 297 us -> none  [body(): total = lax.psum(depth, 'slab')]
    dot_general x22 -> x0, matrix products: 87.1 us -> none  [the longest x1 35.2 us: partial_image(): jnp.einsum('rwk,rwkc->rwc', weight, color, precision=lax.Precision.HIGHEST)]
    ppermute x8 -> x5, starting transfers between devices: 67.8 us -> 12.6 us  [the longest x1 6.71 us: body(): below = lax.ppermute(top, 'slab', back)]
    all_to_all x0 -> x2, blocking collectives: none -> 46.2 us  [the longest x1 24.2 us: body(): depths = lax.all_to_all(depth, 'slab', 0, 0, tiled=True)]
    pallas_call x0 -> x4, Pallas kernels: none -> 24.8 us  [the longest x1 13.5 us: body(): pl.pallas_call(dense_kernel, grid=(steps,), in_specs=[pl.BlockSpec((BLOCK...]
    unnamed x24 -> x12, local copies, waits for them, and re-layouts: 12.6 us -> 3.64 us
  transfers between devices with their start and end apart: 10 -> 5, of which waited for: 5 -> 0; matrix products, arithmetic and copies ran while one was open for 2% -> 2% of each run, Pallas kernels for 0% -> 0%
where the time goes in v1:
time: 89.2 us; the launch traced here: 88.6 us
  blocking collectives  46.2 us (52%)
  Pallas kernels  24.8 us (28%)
  starting transfers between devices  12.6 us (14%)
  local copies, waits for them, and re-layouts  3.64 us (4%)
  between operations  1.33 us (1%)
    all_to_all x1, blocking collectives, body(): depths = lax.all_to_all(depth, 'slab', 0, 0, tiled=True)  24.2 us
    all_to_all x1, blocking collectives, body(): lax.all_to_all(image.reshape(SLABS, STRIP * COLS, C), 'slab', 0, 0, tiled...  22 us
    pallas_call x1, Pallas kernels, body(): pl.pallas_call(dense_kernel, grid=(steps,), in_specs=[pl.BlockSpec((BLOCK...  13.5 us
    pallas_call x1, Pallas kernels, body(): pl.pallas_call(weigh_kernel, grid=(steps,), in_specs=[full(SLABS, GROUPS,...  7.05 us
    ppermute x1, starting transfers between devices, body(): below = lax.ppermute(top, 'slab', back)  6.71 us
    ppermute x1, starting transfers between devices, body(): strip_p = lax.ppermute(strip, 'tile', swap)  3.77 us
    unnamed x12, local copies, waits for them, and re-layouts  3.64 us
    pallas_call x1, Pallas kernels, body(): pl.pallas_call(decode_kernel, in_specs=[vmem] * 10, out_specs=vmem, out_s...  2.27 us
  transfers between devices with their start and end apart: 5, of which 0 were waited for; matrix products, arithmetic and copies ran while one was open for 2% of the time, Pallas kernels for 0%

profile of v1, /device:TPU:1, one launch (start us, length us, event | category | flops | bytes accessed | tf_op | source)
XLA Modules:
  0.0 88.6 jit_solution(4009424380904474495)
XLA Ops:
  1.3 1.5 %copy.14.counts = s32[1,256,16]{2,1,0:T(8,128)} copy(s32[1,256,16]{1,2,0:T(8,128)} %param.13) | data formatting | bytes 32768 | tf_op args[1]
  2.8 13.5 %dense.1 = (bf16[4,128,4096]{2,1,0:T(8,128)(2,1)}, f32[4,32,128]{2,1,0:T(8,128)}, bf16[64,32,128]{2,1,0:T(8,128)(2,1)}) custom-call(f32[4096,256]{1,0:T(8,128)} %bitcast.4, s32[1,256,16]{2,1,0:T(8,128)} %copy.14.counts, f32[1,64,256]{2,1,0:T(8,128)} %w_in.1, f32[1,256]{1,0:T(1,128)} %b_in.1, f32[1,256,128]{2,1,0:T(8,128)} %w_color.1, f32[1,256]{1,0:T(1,128)} %w_density.1, ...), custom_call_target="tpu_custom_call" | custom-call | tf_op jit(solution)/shard_map/dense/pallas_call | solution.py:165
  16.3 24.2 %all_to_all.10.depths = bf16[64,32,128]{2,1,0:T(8,128)(2,1)} all-to-all(bf16[64,32,128]{2,1,0:T(8,128)(2,1)} %get-tuple-element.10), channel_id=1, replica_groups=mesh['slab'=64,'tile'=2] {'slab'}, dimensions={0} | all-to-all | bytes 1048576 | tf_op jit(solution)/shard_map/all_to_all | solution.py:197
  40.5 7.0 %weigh.1 = (bf16[4096,128]{1,0:T(8,128)(2,1)}, f32[1,256,16]{2,1,0:T(8,128)}) custom-call(bf16[64,32,128]{2,1,0:T(8,128)(2,1)} %all_to_all.10.depths, f32[4,32,128]{2,1,0:T(8,128)} %get-tuple-element.11.density, bf16[4,128,4096]{2,1,0:T(8,128)(2,1)} %get-tuple-element.12.color, f32[1,128]{1,0:T(1,128)} %b_color.1), custom_call_target="tpu_custom_call" | custom-call | tf_op jit(solution)/shard_map/weigh/pallas_call | solution.py:199
  47.5 22.0 %all_to_all.11.parts = bf16[64,64,128]{2,1,0:T(8,128)(2,1)} all-to-all(bf16[64,64,128]{2,1,0:T(8,128)(2,1)} %bitcast.5), channel_id=1, replica_groups=mesh['slab'=64,'tile'=2] {'slab'}, dimensions={0} | all-to-all | bytes 2097152 | tf_op jit(solution)/shard_map/all_to_all | solution.py:223
  69.6 2.0 %gathered.1 = (bf16[64,128]{1,0:T(8,128)(2,1)}, bf16[32,128]{1,0:T(8,128)(2,1)}, bf16[32,128]{1,0:T(8,128)(2,1)}) custom-call(bf16[64,64,128]{2,1,0:T(8,128)(2,1)} %all_to_all.11.parts), custom_call_target="tpu_custom_call" | custom-call | tf_op jit(solution)/shard_map/gathered/pallas_call | solution.py:225
  71.6 0.2 collective-permute-start
  71.7 6.7 %collective-permute-start.1 = (bf16[32,128]{1,0:T(8,128)(2,1)}, bf16[32,128]{1,0:T(8,128)(2,1)S(1)}, u32[]{:S(2)}, u32[]{:S(2)}) collective-permute-start(bf16[32,128]{1,0:T(8,128)(2,1)} %get-tuple-element.16), channel_id=1, source_target_pairs={{2,0},{4,2},{6,4},{8,6},{10,8},{12,10},{14,12},{16,14},{18,16},{20... | collective-permute-start | bytes 24584 | tf_op jit(solution)/shard_map/ppermute | solution.py:241
  78.5 3.8 %collective-permute-start.2 = (bf16[64,128]{1,0:T(8,128)(2,1)}, bf16[64,128]{1,0:T(8,128)(2,1)S(1)}, u32[]{:S(2)}, u32[]{:S(2)}) collective-permute-start(bf16[64,128]{1,0:T(8,128)(2,1)} %get-tuple-element.14.strip), channel_id=1, source_target_pairs={{0,1},{1,0},{2,3},{3,2},{4,5},{5,4},{6,7},{7,6},{8,9},{9,8},{10,11... | collective-permute-start | bytes 49160 | tf_op jit(solution)/shard_map/ppermute | solution.py:242
  82.2 0.0 collective-permute-done.above
  82.2 0.0 copy-start.1
  82.2 1.8 %collective-permute-start.3 = (bf16[32,128]{1,0:T(8,128)(2,1)S(1)}, bf16[32,128]{1,0:T(8,128)(2,1)S(1)}, u32[]{:S(2)}, u32[]{:S(2)}) collective-permute-start(bf16[32,128]{1,0:T(8,128)(2,1)S(1)} %collective-permute-done.above), channel_id=1, source_target_pairs={{0,1},{1,0},{2,3},{3,2},{4,5},{5,4},{6,7},{7,6},{8,9},{9,8},{10,11... | collective-permute-start | bytes 24584 | tf_op jit(solution)/shard_map/ppermute | solution.py:243
  84.1 0.0 collective-permute-done.1.below
  84.1 0.0 copy-start.2
  84.1 0.1 collective-permute-start.4
  84.2 1.6 %copy.15 = f32[1,256,16]{1,2,0:T(8,128)} copy(f32[1,256,16]{2,1,0:T(8,128)} %get-tuple-element.19) | data formatting | bytes 32768
  85.7 0.0 collective-permute-done.3.above_p
  85.7 0.0 copy-start.3
  85.7 0.0 collective-permute-done.4.below_p
  85.8 0.0 copy-start.4
  85.8 0.0 collective-permute-done.2.strip_p
  85.8 0.0 copy-start
  85.8 0.0 copy-done.1
  85.8 0.0 copy-done.2
  85.8 0.5 copy-done.3
  86.3 0.0 copy-done.4
  86.3 0.0 copy-done
  86.4 2.3 %decode.1 = bf16[4,16,128]{2,1,0:T(8,128)(2,1)} custom-call(bf16[64,128]{1,0:T(8,128)(2,1)} %get-tuple-element.14.strip, bf16[32,128]{1,0:T(8,128)(2,1)} %copy-done.1, bf16[32,128]{1,0:T(8,128)(2,1)} %copy-done.2, bf16[64,128]{1,0:T(8,128)(2,1)} %copy-done, bf16[32,128]{1,0:T(8,128)(2,1)} %copy-done.3, bf16[32,128]{1,0:T(8,128)(2,1)} %copy-done.4, ...), custom_call_target="tpu_custom_call" | custom-call | tf_op jit(solution)/shard_map/decode/pallas_call | solution.py:246
Async XLA Ops:
  71.6 10.7 %collective-permute-start = (bf16[32,128]{1,0:T(8,128)(2,1)}, bf16[32,128]{1,0:T(8,128)(2,1)S(1)}, u32[]{:S(2)}, u32[]{:S(2)}) collective-permute-start(bf16[32,128]{1,0:T(8,128)(2,1)} %get-tuple-element.15), channel_id=1, source_target_pairs={{0,2},{2,4},{4,6},{6,8},{8,10},{10,12},{12,14},{14,16},{16,18},{18... | collective-permute-start | bytes 24584 | tf_op jit(solution)/shard_map/ppermute | solution.py:240
  71.7 12.3 %collective-permute-start.1 = (bf16[32,128]{1,0:T(8,128)(2,1)}, bf16[32,128]{1,0:T(8,128)(2,1)S(1)}, u32[]{:S(2)}, u32[]{:S(2)}) collective-permute-start(bf16[32,128]{1,0:T(8,128)(2,1)} %get-tuple-element.16), channel_id=1, source_target_pairs={{2,0},{4,2},{6,4},{8,6},{10,8},{12,10},{14,12},{16,14},{18,16},{20... | collective-permute-start | bytes 24584 | tf_op jit(solution)/shard_map/ppermute | solution.py:241
  78.5 7.3 %collective-permute-start.2 = (bf16[64,128]{1,0:T(8,128)(2,1)}, bf16[64,128]{1,0:T(8,128)(2,1)S(1)}, u32[]{:S(2)}, u32[]{:S(2)}) collective-permute-start(bf16[64,128]{1,0:T(8,128)(2,1)} %get-tuple-element.14.strip), channel_id=1, source_target_pairs={{0,1},{1,0},{2,3},{3,2},{4,5},{5,4},{6,7},{7,6},{8,9},{9,8},{10,11... | collective-permute-start | bytes 49160 | tf_op jit(solution)/shard_map/ppermute | solution.py:242
  82.2 3.6 %copy-start.1 = (bf16[32,128]{1,0:T(8,128)(2,1)}, bf16[32,128]{1,0:T(8,128)(2,1)S(1)}, u32[]{:S(2)}) copy-start(bf16[32,128]{1,0:T(8,128)(2,1)S(1)} %collective-permute-done.above) | copy-start | bytes 24580
  82.2 3.5 %collective-permute-start.3 = (bf16[32,128]{1,0:T(8,128)(2,1)S(1)}, bf16[32,128]{1,0:T(8,128)(2,1)S(1)}, u32[]{:S(2)}, u32[]{:S(2)}) collective-permute-start(bf16[32,128]{1,0:T(8,128)(2,1)S(1)} %collective-permute-done.above), channel_id=1, source_target_pairs={{0,1},{1,0},{2,3},{3,2},{4,5},{5,4},{6,7},{7,6},{8,9},{9,8},{10,11... | collective-permute-start | bytes 24584 | tf_op jit(solution)/shard_map/ppermute | solution.py:243
  84.1 1.7 %copy-start.2 = (bf16[32,128]{1,0:T(8,128)(2,1)}, bf16[32,128]{1,0:T(8,128)(2,1)S(1)}, u32[]{:S(2)}) copy-start(bf16[32,128]{1,0:T(8,128)(2,1)S(1)} %collective-permute-done.1.below) | copy-start | bytes 24580
  84.1 1.7 %collective-permute-start.4 = (bf16[32,128]{1,0:T(8,128)(2,1)S(1)}, bf16[32,128]{1,0:T(8,128)(2,1)S(1)}, u32[]{:S(2)}, u32[]{:S(2)}) collective-permute-start(bf16[32,128]{1,0:T(8,128)(2,1)S(1)} %collective-permute-done.1.below), channel_id=1, source_target_pairs={{0,1},{1,0},{2,3},{3,2},{4,5},{5,4},{6,7},{7,6},{8,9},{9,8},{10,11... | collective-permute-start | bytes 24584 | tf_op jit(solution)/shard_map/ppermute | solution.py:244
  85.7 0.6 copy-start.3
  85.8 0.6 copy-start.4
  85.8 0.6 copy-start

commit v2 on v1

v2 whole, which is shorter than its diff:
```python
import jax
import jax.numpy as jnp
from jax import lax
from jax.experimental import pallas as pl
from jax.experimental.pallas import tpu as pltpu
from jax.sharding import PartitionSpec as P

F = 64
HID = 256
C = 128
K = 4
SLABS = 64
ROWS = 256
COLS = 16
RAYS = ROWS * COLS
LANES = 128
GROUPS = RAYS // LANES
BLOCK = 512
PER = BLOCK // LANES
STEPS = RAYS // BLOCK
HEAD = C + 16
STRIP = 4
BF = jnp.bfloat16
F32 = jnp.float32

NT = (((1,), (1,)), ((), ()))


def column(row, lanes):
    return jnp.broadcast_to(row, (lanes, row.shape[1])).T


def dense_kernel(samples, counts, w_in, b_in, w_color, w_density, b_density,
                 color, density, depth, x, w_s, b_s, c_s, logit, turn_s, sems):
    def fetch(step):
        return pltpu.make_async_copy(samples.at[pl.ds(step * BLOCK, BLOCK), :], x.at[step], sems.at[step])

    for step in range(STEPS):
        fetch(step).start()

    turned = w_in[0].T.astype(BF)
    w_s[...] = jnp.zeros_like(w_s)
    for k in range(K):
        w_s[k * HID:(k + 1) * HID, k * F:(k + 1) * F] = turned
    b_s[...] = column(b_in[...], LANES)
    c_s[:C, :] = w_color[0].T.astype(BF)
    head = w_density[...]
    coarse = head.astype(BF)
    fine = (head - coarse.astype(F32)).astype(BF)
    place = lax.broadcasted_iota(jnp.int32, (HEAD - C, HID), 0)
    c_s[C:, :] = jnp.where(
        place == 0, coarse.astype(F32), jnp.where(place == 1, fine.astype(F32), 0.0)
    ).astype(BF)

    def one(step, _):
        fetch(step).wait()
        rays = x[step].astype(BF)
        bias = jnp.concatenate([b_s[...]] * PER, axis=1)

        def first(k):
            return lax.dot_general(w_s[k * HID:(k + 1) * HID, :], rays, NT, preferred_element_type=F32)

        hidden = first(0)
        for k in range(K):
            ahead = first(k + 1) if k + 1 < K else None
            lit = jnp.maximum((hidden + bias).astype(BF), jnp.zeros((), BF))
            made = jnp.dot(c_s[...], lit, preferred_element_type=F32)
            color[k, :, pl.ds(step * BLOCK, BLOCK)] = made[:C].astype(BF)
            before = made[C:C + 1] + made[C + 1:C + 2]
            for g in range(PER):
                logit[k, pl.ds(step * PER + g, 1), :] = before[:, g * LANES:(g + 1) * LANES]
            hidden = ahead
        return 0

    lax.fori_loop(0, STEPS, one, 0)

    turn_s[...] = counts[0].astype(F32).T
    live = jnp.concatenate([turn_s[pl.ds(a, GROUPS, stride=8), :] for a in range(8)], axis=1)
    total = jnp.zeros((GROUPS, LANES), F32)
    for k in range(K):
        pre = logit[k] + b_density[0]
        soft = jnp.maximum(pre, 0.0) + jnp.log1p(jnp.exp(-jnp.abs(pre)))
        soft = jnp.where(live > k, soft, 0.0)
        density[k] = soft
        total = total + soft
    depth[...] = jnp.broadcast_to(total.astype(BF)[None], depth.shape)


def weigh_kernel(depths, density, color, b_color, image, front, w_s, b_s, turn_s):
    place = lax.axis_index("slab")
    b_s[...] = column(b_color[...], LANES)

    def add(turn, state):
        total, ahead = state
        one = depths[turn].astype(F32)
        return total + one, ahead + jnp.where(turn < place, one, 0.0)

    zero = jnp.zeros((GROUPS, LANES), F32)
    total, ahead = lax.fori_loop(0, SLABS, add, (zero, zero), unroll=8)
    ahead = ahead / total
    for a in range(8):
        turn_s[pl.ds(a, GROUPS, stride=8), :] = ahead[:, a * COLS:(a + 1) * COLS]
    front[0] = turn_s[...].T
    passed = ahead
    for k in range(K):
        scaled = density[k] / total
        w_s[k] = jnp.exp(-passed) * (1.0 - jnp.exp(-scaled))
        passed = passed + scaled

    def one(step, _):
        for g in range(PER):
            at = pl.ds(step * PER + g, 1)
            lanes = pl.ds((step * PER + g) * LANES, LANES)
            weights = [w_s[k, at, :] for k in range(K)]
            part = b_s[...] * (weights[0] + weights[1] + weights[2] + weights[3])
            for k in range(K):
                part = part + color[k, :, lanes].astype(F32) * weights[k]
            image[lanes, :] = part.T.astype(BF)
        return 0

    lax.fori_loop(0, STEPS, one, 0)


def sum_kernel(parts, strip, top, bottom):
    total = jnp.zeros((STRIP * COLS, C), F32)

    def add(turn, state):
        return state + parts[turn].astype(F32)

    total = lax.fori_loop(0, SLABS, add, total, unroll=8).astype(BF)
    strip[...] = total
    top[...] = total[:2 * COLS]
    bottom[...] = total[2 * COLS:]


PITCH = 32
EDGE = 8


def taps(field, rows):
    flat = field.reshape(-1, C)
    span = flat.shape[0]
    shifted = [pltpu.roll(flat, 1, 0).astype(BF), flat.astype(BF), pltpu.roll(flat, span - 1, 0).astype(BF)]
    return jnp.concatenate(
        [s[PITCH * r:PITCH * (r + rows)] for r in range(3) for s in shifted], axis=1
    )


def decode_kernel(strip, above, below, strip_p, above_p, below_p, conv_a, bias_a, conv_b, bias_b, out, patch):
    place = lax.axis_index("slab")
    tile = lax.axis_index("tile")
    first = place == 0
    last = place == SLABS - 1

    def whole(up, mid, down):
        up = jnp.where(first, 0.0, up[...].astype(F32))
        down = jnp.where(last, 0.0, down[...].astype(F32))
        return jnp.concatenate([up, mid[...].astype(F32), down], axis=0).reshape(STRIP + 4, COLS, C)

    own = whole(above, strip, below)
    other = whole(above_p, strip_p, below_p)
    patch[...] = jnp.zeros_like(patch)
    patch[:, EDGE:EDGE + COLS, :] = own
    patch[:, EDGE - 2:EDGE, :] = jnp.where(tile == 0, 0.0, other[:, COLS - 2:, :])
    patch[:, EDGE + COLS:EDGE + COLS + 2, :] = jnp.where(tile == 0, other[:, :2, :], 0.0)
    rows = STRIP + 2
    made = jnp.dot(taps(patch[...], rows), conv_a[...].reshape(9 * C, C), preferred_element_type=F32)
    made = jnp.maximum(made + bias_a[...], 0.0).astype(BF).astype(F32).reshape(rows, PITCH, C)
    row = lax.broadcasted_iota(jnp.int32, made.shape, 0) + (place * STRIP - 1)
    col = lax.broadcasted_iota(jnp.int32, made.shape, 1) + (tile * COLS - EDGE)
    inside = (row >= 0) & (row < ROWS) & (col >= 0) & (col < 2 * COLS)
    made = jnp.where(inside, made, 0.0)
    done = jnp.dot(taps(made, STRIP), conv_b[...].reshape(9 * C, C), preferred_element_type=F32) + bias_b[...]
    out[...] = done.reshape(STRIP, PITCH, C)[:, EDGE:EDGE + COLS, :].astype(BF)


def call(kernel, name, out, scratch=(), spaces=(), limit=4, given=0):
    vmem = pl.BlockSpec(memory_space=pltpu.VMEM)
    return pl.pallas_call(
        kernel,
        in_specs=[pl.BlockSpec(memory_space=dict(spaces).get(i, pltpu.VMEM)) for i in range(given)],
        out_specs=[vmem] * len(out),
        out_shape=out,
        scratch_shapes=list(scratch),
        compiler_params=pltpu.CompilerParams(vmem_limit_bytes=limit << 20),
        name=name,
    )


def body(samples, counts, w_in, b_in, w_color, b_color, w_density, b_density, conv_a, bias_a, conv_b, bias_b):
    shape = jax.ShapeDtypeStruct
    color, density, depth = call(
        dense_kernel,
        "dense",
        [
            shape((K, C, RAYS), BF),
            shape((K, GROUPS, LANES), F32),
            shape((SLABS, GROUPS, LANES), BF),
        ],
        [
            pltpu.VMEM((STEPS, BLOCK, K * F), F32),
            pltpu.VMEM((K * HID, K * F), BF),
            pltpu.VMEM((HID, LANES), F32),
            pltpu.VMEM((HEAD, HID), BF),
            pltpu.VMEM((K, GROUPS, LANES), F32),
            pltpu.VMEM((ROWS, COLS), F32),
            pltpu.SemaphoreType.DMA((STEPS,)),
        ],
        {0: pltpu.HBM, 6: pltpu.SMEM},
        16,
        7,
    )(pltpu.with_memory_space_constraint(samples.reshape(RAYS, K * F), pltpu.HBM), counts.transpose(0, 2, 1), w_in, b_in, w_color, w_density, b_density)

    depths = lax.all_to_all(depth, "slab", 0, 0, tiled=True)

    image, front = call(
        weigh_kernel,
        "weigh",
        [shape((RAYS, C), BF), shape((1, COLS, ROWS), F32)],
        [
            pltpu.VMEM((K, GROUPS, LANES), F32),
            pltpu.VMEM((C, LANES), F32),
            pltpu.VMEM((ROWS, COLS), F32),
        ],
        given=4,
        limit=16,
    )(depths, density, color, b_color)
    front = front.transpose(0, 2, 1)

    parts = lax.all_to_all(image.reshape(SLABS, STRIP * COLS, C), "slab", 0, 0, tiled=True)

    strip, top, bottom = call(
        sum_kernel,
        "gathered",
        [shape((STRIP * COLS, C), BF), shape((2 * COLS, C), BF), shape((2 * COLS, C), BF)],
        given=1,
        limit=8,
    )(parts)

    onward = [(i, (i + 1) % SLABS) for i in range(SLABS)]
    back = [(j, i) for i, j in onward]
    swap = [(0, 1), (1, 0)]
    above = lax.ppermute(bottom, "slab", onward)
    below = lax.ppermute(top, "slab", back)
    strip_p = lax.ppermute(strip, "tile", swap)
    above_p = lax.ppermute(above, "tile", swap)
    below_p = lax.ppermute(below, "tile", swap)

    (decoded,) = call(
        decode_kernel,
        "decode",
        [shape((STRIP, COLS, C), BF)],
        [pltpu.VMEM((STRIP + 4, PITCH, C), F32)],
        given=10,
        limit=8,
    )(strip, above, below, strip_p, above_p, below_p, conv_a, bias_a.reshape(1, C), conv_b, bias_b.reshape(1, C))
    return decoded, front


def solution(mesh):
    in_specs = (
        P("slab", None, "tile", None),
        P("slab", None, "tile"),
        P("slab", None, None),
        P("slab", None),
        P("slab", None, None),
        P("slab", None),
        P("slab", None),
        P("slab"),
        P(),
        P(),
        P(),
        P(),
    )
    out_specs = (P("slab", "tile", None), P("slab", None, "tile"))
    return jax.shard_map(body, mesh=mesh, in_specs=in_specs, out_specs=out_specs, check_vma=False)
```

time: 89.2 us -> 79.8 us (0.89)
  Pallas kernels: 24.8 us -> 15.9 us
  blocking collectives: 46.2 us -> 44.4 us
  waiting for transfers between devices: 0.01 us -> 1.18 us
    pallas_call x4, Pallas kernels: 24.8 us -> 15.9 us  [the longest x1 11.8 us: body(): call(dense_kernel, 'dense', [shape((K, C, RAYS), BF), shape((K, GROUPS, L...]
    all_to_all x1, blocking collectives: 22 us -> 20.5 us  [body(): lax.all_to_all(image.reshape(SLABS, STRIP * COLS, C), 'slab', 0, 0, tiled...]
    unnamed x12 -> x20, local copies, waits for them, and re-layouts: 3.64 us -> 3.83 us
  transfers between devices with their start and end apart: 5 -> 5, of which waited for: 0 -> 2; matrix products, arithmetic and copies ran while one was open for 2% -> 0% of each run, Pallas kernels for 0% -> 0%
where the time goes in v2:
time: 79.8 us; the launch traced here: 79.5 us
  blocking collectives  44.4 us (56%)
  Pallas kernels  15.9 us (20%)
  starting transfers between devices  12.7 us (16%)
  local copies, waits for them, and re-layouts  3.83 us (5%)
  between operations  1.37 us (2%)
  waiting for transfers between devices  1.18 us (1%)
    all_to_all x1, blocking collectives, body(): depths = lax.all_to_all(depth, 'slab', 0, 0, tiled=True)  23.9 us
    all_to_all x1, blocking collectives, body(): lax.all_to_all(image.reshape(SLABS, STRIP * COLS, C), 'slab', 0, 0, tiled...  20.5 us
    pallas_call x1, Pallas kernels, body(): call(dense_kernel, 'dense', [shape((K, C, RAYS), BF), shape((K, GROUPS, L...  11.8 us
    ppermute x1, starting transfers between devices, body(): below = lax.ppermute(top, 'slab', back)  6.43 us
    ppermute x1, starting transfers between devices, body(): strip_p = lax.ppermute(strip, 'tile', swap)  4.13 us
    unnamed x20, local copies, waits for them, and re-layouts  3.83 us
    pallas_call x1, Pallas kernels, body(): call(weigh_kernel, 'weigh', [shape((RAYS, C), BF), shape((1, COLS, ROWS),...  2.85 us
    ppermute x1, starting transfers between devices, body(): above_p = lax.ppermute(above, 'tile', swap)  1.62 us
  transfers between devices with their start and end apart: 5, of which 2 were waited for; matrix products, arithmetic and copies ran while one was open for 0% of the time, Pallas kernels for 0%

profile of v2, /device:TPU:1, one launch (start us, length us, event | category | flops | bytes accessed | tf_op | source)
XLA Modules:
  0.0 79.5 jit_solution(6691690260708343180)
XLA Ops:
  0.6 0.0 copy-start.7
  1.3 0.0 copy-start.2
  1.3 0.9 %copy-done.2 = f32[1,256,128]{2,1,0:T(8,128)S(1)} copy-done((f32[1,256,128]{2,1,0:T(8,128)S(1)}, f32[1,256,128]{2,1,0:T(8,128)}, u32[]{:S(2)}) %copy-start.2) | copy-done | bytes 131096
  2.2 0.0 copy-start.3
  2.2 0.8 %copy-done.3 = f32[1,64,256]{2,1,0:T(8,128)S(1)} copy-done((f32[1,64,256]{2,1,0:T(8,128)S(1)}, f32[1,64,256]{2,1,0:T(8,128)}, u32[]{:S(2)}) %copy-start.3) | copy-done | bytes 65560
  3.0 0.0 copy-start.4
  3.0 0.7 copy-done.4
  3.8 0.0 copy-start.5
  3.8 0.7 copy-done.5
  4.4 0.0 copy-start.6
  4.4 0.7 copy-done.6
  5.1 11.8 %dense.1 = (bf16[4,128,4096]{2,1,0:T(8,128)(2,1)S(1)}, f32[4,32,128]{2,1,0:T(8,128)S(1)}, bf16[64,32,128]{2,1,0:T(8,128)(2,1)S(1)}) custom-call(f32[4096,256]{1,0:T(8,128)} %bitcast.10, s32[1,16,256]{2,1,0:T(8,128)S(1)} %bitcast.7, f32[1,64,256]{2,1,0:T(8,128)S(1)} %copy-done.3, f32[1,256]{1,0:T(1,128)S(1)} %copy-done.5, f32[1,256,128]{2,1,0:T(8,128)S(1)} %copy-done.2, ...), custom_call_target="tpu_custom_call" | custom-call | tf_op jit(solution)/shard_map/dense/pallas_call | solution.py:192
  17.0 23.9 %all_to_all.10.depths = bf16[64,32,128]{2,1,0:T(8,128)(2,1)S(1)} all-to-all(bf16[64,32,128]{2,1,0:T(8,128)(2,1)S(1)} %get-tuple-element.10), channel_id=1, replica_groups=mesh['slab'=64,'tile'=2] {'slab'}, dimensions={0} | all-to-all | bytes 1048576 | tf_op jit(solution)/shard_map/all_to_all | solution.py:214
  40.9 0.0 copy-start
  40.9 0.0 copy-start.1
  40.9 0.0 copy-start.8
  40.9 0.0 copy-start.9
  40.9 0.0 copy-done.7
  40.9 2.9 %weigh.1 = (bf16[4096,128]{1,0:T(8,128)(2,1)S(1)}, f32[1,16,256]{2,1,0:T(8,128)}) custom-call(bf16[64,32,128]{2,1,0:T(8,128)(2,1)S(1)} %all_to_all.10.depths, f32[4,32,128]{2,1,0:T(8,128)S(1)} %get-tuple-element.11.density, bf16[4,128,4096]{2,1,0:T(8,128)(2,1)S(1)} %get-tuple-element.12.color, f32[1,128]{1,0:T(1,128)S(1)} %copy-done.7), custom_call_target="tpu_custom_call" | custom-call | tf_op jit(solution)/shard_map/weigh/pallas_call | solution.py:216
  43.7 20.5 %all_to_all.11.parts = bf16[64,64,128]{2,1,0:T(8,128)(2,1)S(1)} all-to-all(bf16[64,64,128]{2,1,0:T(8,128)(2,1)S(1)} %bitcast.6), channel_id=1, replica_groups=mesh['slab'=64,'tile'=2] {'slab'}, dimensions={0} | all-to-all | bytes 2097152 | tf_op jit(solution)/shard_map/all_to_all | solution.py:230
  64.3 0.2 gathered.1
  64.4 0.5 collective-permute-start
  65.0 6.4 %collective-permute-start.1 = (bf16[32,128]{1,0:T(8,128)(2,1)S(1)}, bf16[32,128]{1,0:T(8,128)(2,1)S(1)}, u32[]{:S(2)}, u32[]{:S(2)}) collective-permute-start(bf16[32,128]{1,0:T(8,128)(2,1)S(1)} %get-tuple-element.16), channel_id=1, source_target_pairs={{2,0},{4,2},{6,4},{8,6},{10,8},{12,10},{14,12},{16,14},{18,16},{20... | collective-permute-start | bytes 24584 | tf_op jit(solution)/shard_map/ppermute | solution.py:244
  71.4 4.1 %collective-permute-start.2 = (bf16[64,128]{1,0:T(8,128)(2,1)S(1)}, bf16[64,128]{1,0:T(8,128)(2,1)S(1)}, u32[]{:S(2)}, u32[]{:S(2)}) collective-permute-start(bf16[64,128]{1,0:T(8,128)(2,1)S(1)} %get-tuple-element.14.strip), channel_id=1, source_target_pairs={{0,1},{1,0},{2,3},{3,2},{4,5},{5,4},{6,7},{7,6},{8,9},{9,8},{10,11... | collective-permute-start | bytes 49160 | tf_op jit(solution)/shard_map/ppermute | solution.py:245
  75.5 0.0 collective-permute-done.above
  75.5 1.6 %collective-permute-start.3 = (bf16[32,128]{1,0:T(8,128)(2,1)S(1)}, bf16[32,128]{1,0:T(8,128)(2,1)S(1)}, u32[]{:S(2)}, u32[]{:S(2)}) collective-permute-start(bf16[32,128]{1,0:T(8,128)(2,1)S(1)} %collective-permute-done.above), channel_id=1, source_target_pairs={{0,1},{1,0},{2,3},{3,2},{4,5},{5,4},{6,7},{7,6},{8,9},{9,8},{10,11... | collective-permute-start | bytes 24584 | tf_op jit(solution)/shard_map/ppermute | solution.py:246
  77.2 0.0 collective-permute-done.1.below
  77.2 0.0 collective-permute-start.4
  77.2 0.8 %collective-permute-done.3.above_p = bf16[32,128]{1,0:T(8,128)(2,1)S(1)} collective-permute-done((bf16[32,128]{1,0:T(8,128)(2,1)S(1)}, bf16[32,128]{1,0:T(8,128)(2,1)S(1)}, u32[]{:S(2)}, u32[]{:S(2)}) %collective-permute-start.3) | collective-permute-done | bytes 8224 | tf_op jit(solution)/shard_map/ppermute | solution.py:246
  78.0 0.3 collective-permute-done.4.below_p
  78.3 0.0 collective-permute-done.2.strip_p
  78.3 0.0 copy-done
  78.3 0.0 copy-done.1
  78.3 0.0 copy-done.8
  78.4 0.0 copy-done.9
  78.4 1.1 %decode.1 = bf16[4,16,128]{2,1,0:T(8,128)(2,1)} custom-call(bf16[64,128]{1,0:T(8,128)(2,1)S(1)} %get-tuple-element.14.strip, bf16[32,128]{1,0:T(8,128)(2,1)S(1)} %collective-permute-done.above, bf16[32,128]{1,0:T(8,128)(2,1)S(1)} %collective-permute-done.1.below, bf16[64,128]{1,0:T(8,128)(2,1)S(1)} %collective-permute-done.2.strip_p, ...), custom_call_target="tpu_custom_call" | custom-call | tf_op jit(solution)/shard_map/decode/pallas_call | solution.py:249
Async XLA Ops:
  0.6 40.2 %copy-start.7 = (f32[1,128]{1,0:T(1,128)S(1)}, f32[1,128]{1,0:T(1,128)}, u32[]{:S(2)}) copy-start(f32[1,128]{1,0:T(1,128)} %b_color.1) | copy-start | bytes 1540
  1.3 0.9 %copy-start.2 = (f32[1,256,128]{2,1,0:T(8,128)S(1)}, f32[1,256,128]{2,1,0:T(8,128)}, u32[]{:S(2)}) copy-start(f32[1,256,128]{2,1,0:T(8,128)} %w_color.1) | copy-start | bytes 393220
  2.2 0.8 %copy-start.3 = (f32[1,64,256]{2,1,0:T(8,128)S(1)}, f32[1,64,256]{2,1,0:T(8,128)}, u32[]{:S(2)}) copy-start(f32[1,64,256]{2,1,0:T(8,128)} %w_in.1) | copy-start | bytes 196612
  3.0 0.7 copy-start.4
  3.8 0.7 copy-start.5
  4.4 0.7 copy-start.6
  40.9 37.5 %copy-start = (bf16[3,3,128,128]{3,2,1,0:T(8,128)(2,1)S(1)}, bf16[3,3,128,128]{3,2,1,0:T(8,128)(2,1)}, u32[]{:S(2)}) copy-start(bf16[3,3,128,128]{3,2,1,0:T(8,128)(2,1)} %conv_a.1) | copy-start | bytes 884740
  40.9 37.5 %copy-start.1 = (bf16[3,3,128,128]{3,2,1,0:T(8,128)(2,1)S(1)}, bf16[3,3,128,128]{3,2,1,0:T(8,128)(2,1)}, u32[]{:S(2)}) copy-start(bf16[3,3,128,128]{3,2,1,0:T(8,128)(2,1)} %conv_b.1) | copy-start | bytes 884740
  40.9 37.5 %copy-start.8 = (f32[128]{0:T(128)S(1)}, f32[128]{0:T(128)}, u32[]{:S(2)}) copy-start(f32[128]{0:T(128)} %param.21) | copy-start | bytes 1540
  40.9 37.5 %copy-start.9 = (f32[128]{0:T(128)S(1)}, f32[128]{0:T(128)}, u32[]{:S(2)}) copy-start(f32[128]{0:T(128)} %param.23) | copy-start | bytes 1540
  64.4 11.1 %collective-permute-start = (bf16[32,128]{1,0:T(8,128)(2,1)S(1)}, bf16[32,128]{1,0:T(8,128)(2,1)S(1)}, u32[]{:S(2)}, u32[]{:S(2)}) collective-permute-start(bf16[32,128]{1,0:T(8,128)(2,1)S(1)} %get-tuple-element.15), channel_id=1, source_target_pairs={{0,2},{2,4},{4,6},{6,8},{8,10},{10,12},{12,14},{14,16},{16,18},{18... | collective-permute-start | bytes 24584 | tf_op jit(solution)/shard_map/ppermute | solution.py:243
  65.0 12.2 %collective-permute-start.1 = (bf16[32,128]{1,0:T(8,128)(2,1)S(1)}, bf16[32,128]{1,0:T(8,128)(2,1)S(1)}, u32[]{:S(2)}, u32[]{:S(2)}) collective-permute-start(bf16[32,128]{1,0:T(8,128)(2,1)S(1)} %get-tuple-element.16), channel_id=1, source_target_pairs={{2,0},{4,2},{6,4},{8,6},{10,8},{12,10},{14,12},{16,14},{18,16},{20... | collective-permute-start | bytes 24584 | tf_op jit(solution)/shard_map/ppermute | solution.py:244
  71.4 6.9 %collective-permute-start.2 = (bf16[64,128]{1,0:T(8,128)(2,1)S(1)}, bf16[64,128]{1,0:T(8,128)(2,1)S(1)}, u32[]{:S(2)}, u32[]{:S(2)}) collective-permute-start(bf16[64,128]{1,0:T(8,128)(2,1)S(1)} %get-tuple-element.14.strip), channel_id=1, source_target_pairs={{0,1},{1,0},{2,3},{3,2},{4,5},{5,4},{6,7},{7,6},{8,9},{9,8},{10,11... | collective-permute-start | bytes 49160 | tf_op jit(solution)/shard_map/ppermute | solution.py:245
  75.5 2.5 %collective-permute-start.3 = (bf16[32,128]{1,0:T(8,128)(2,1)S(1)}, bf16[32,128]{1,0:T(8,128)(2,1)S(1)}, u32[]{:S(2)}, u32[]{:S(2)}) collective-permute-start(bf16[32,128]{1,0:T(8,128)(2,1)S(1)} %collective-permute-done.above), channel_id=1, source_target_pairs={{0,1},{1,0},{2,3},{3,2},{4,5},{5,4},{6,7},{7,6},{8,9},{9,8},{10,11... | collective-permute-start | bytes 24584 | tf_op jit(solution)/shard_map/ppermute | solution.py:246
  77.2 1.2 %collective-permute-start.4 = (bf16[32,128]{1,0:T(8,128)(2,1)S(1)}, bf16[32,128]{1,0:T(8,128)(2,1)S(1)}, u32[]{:S(2)}, u32[]{:S(2)}) collective-permute-start(bf16[32,128]{1,0:T(8,128)(2,1)S(1)} %collective-permute-done.1.below), channel_id=1, source_target_pairs={{0,1},{1,0},{2,3},{3,2},{4,5},{5,4},{6,7},{7,6},{8,9},{9,8},{10,11... | collective-permute-start | bytes 24584 | tf_op jit(solution)/shard_map/ppermute | solution.py:247
